TPU v7x, 256 devices: a whole 4x4x8 slice. The times are simulated.
256 devices in a mesh: mem: 4 (over y_hi, core), strip: 64 (over x, y_lo, z).
Axes of the slice: x: 4, y: 4 (y_hi: 2, y_lo: 2; y = y_hi * 2 + y_lo), z: 8, core: 2. Of those that a mesh axis runs over, the one named last changes fastest.
Arguments:
- gradient: float32 [8, 2048, 1024], P('mem', 'strip'), may hold values from -6 to 6
- perturbations: bfloat16 [64, 8, 2048, 1024], P('mem', None, 'strip'), may hold values from -6 to 6
- counts: int32 [2048, 1024], P('strip'), may hold values from 1 to 4, as said below
Outputs:
- increment: float32 [8, 2048, 1024], P('mem', 'strip')
Inputs may be any that keep to these rules, and one draw needn't show every extreme that they name: `counts`: counts are drawn band by band of 32 rows along the first dimension, each band under a cap of its own; some cell reaches 4.
All inputs are finite; a program needn't handle non-finite values.
Results may differ from a plain program's by a relative error of at most 0.0003.
Values sent between devices are 32-bit elements; how exact they have to be, the bound alone decides.
A program may use at most 64 MiB of HBM per device.

v0:
```python
import math

import jax
import jax.numpy as jnp
from jax import lax
from jax.sharding import PartitionSpec as P

SLOTS = 2
VARS = 4
FIELDS = 8
SWEEPS = 4


COEFF_X = 0.35
COEFF_Y = 0.12


def with_halo(x, sides, width):
    for axis, dim in sides:
        size, length = (lax.axis_size(axis), x.shape[dim])
        up = [(i, (i + 1) % size) for i in range(size - 1)]
        down = [(j, i) for i, j in up]
        last = lax.slice_in_dim(x, length - width, length, axis=dim)
        initial = lax.slice_in_dim(x, 0, width, axis=dim)
        before = lax.ppermute(last, axis, up)
        after = lax.ppermute(initial, axis, down)
        x = jnp.concatenate([before, x, after], axis=dim)
    return x


def split_up(x, dim, size):
    before, after = (x.shape[:dim], x.shape[dim + 1 :])
    return jnp.moveaxis(x.reshape(*before, size, -1, *after), dim, 0)


def sent_and_summed(x, axis, dim):
    blocks = split_up(x, dim, lax.axis_size(axis))
    arrived = lax.all_to_all(blocks, axis, split_axis=0, concat_axis=0, tiled=True)
    return arrived.sum(axis=0)


def joined_along(blocks, dim):
    blocks = jnp.moveaxis(blocks, 0, dim)
    shape = blocks.shape
    return blocks.reshape(*shape[:dim], shape[dim] * shape[dim + 1], *shape[dim + 2 :])


def copy_for_each(x, axis):
    copies = jnp.broadcast_to(x, (lax.axis_size(axis), *x.shape))
    return lax.all_to_all(copies, axis, split_axis=0, concat_axis=0, tiled=True)


def collect(x, axis, dim):
    return joined_along(copy_for_each(x, axis), dim)


def advance(padded_x, active):
    padded = jnp.pad(padded_x, ((0, 0), (0, 0), (0, 0), (1, 1)))
    centre = padded[:, :, 1:-1, 1:-1]
    along_x = padded[:, :, 2:, 1:-1] + padded[:, :, :-2, 1:-1] - 2.0 * centre
    along_y = padded[:, :, 1:-1, 2:] + padded[:, :, 1:-1, :-2] - 2.0 * centre
    return centre + active * (COEFF_X * along_x + COEFF_Y * along_y)


def sweep_once(state_field, active):
    padded_x = jnp.pad(state_field, ((0, 0), (0, 0), (1, 1), (0, 0)))
    return advance(padded_x, active)


def diffuse(state_field, counts):
    cells_x = counts.shape[0]
    extended = with_halo(state_field, (("strip", 2),), SWEEPS)
    limits = with_halo(counts, (("strip", 0),), SWEEPS)
    for sweep_index in range(SWEEPS):
        extended = sweep_once(extended, (limits > sweep_index).astype(jnp.float32))
    return extended[:, :, SWEEPS : SWEEPS + cells_x]


def settle(projected, pert_block, counts, own_rows, norm_scale):
    smooth = diffuse(projected, counts)
    first_row = jnp.int32(0)
    results = []
    for row_offset in range(own_rows * lax.axis_size("mem")):
        row_index = first_row + row_offset
        slot_index = row_index // VARS
        pert_row = lax.dynamic_index_in_dim(pert_block, row_index, 1, keepdims=False).astype(
            jnp.float32
        )
        chosen = lax.dynamic_index_in_dim(smooth, slot_index, 1, keepdims=False)
        results.append(jnp.sum(pert_row * chosen, axis=0) * norm_scale)
    return sent_and_summed(jnp.stack(results, axis=0), "mem", 0)


def per_device(gradient, perturbations, counts):
    members = perturbations.shape[0]
    cells_x, cells_y = counts.shape
    own_rows = gradient.shape[0]
    norm_scale = 1.0 / math.sqrt(members * lax.axis_size("mem") * FIELDS)
    zero_sum = jnp.zeros((members, SLOTS, cells_x, cells_y), jnp.float32)
    running = zero_sum
    piece_rows = collect(gradient, "mem", 0)
    first_row = jnp.int32(0)
    for row_offset in range(piece_rows.shape[0]):
        row_index = first_row + row_offset
        slot_index = row_index // VARS
        pert_row = lax.dynamic_index_in_dim(perturbations, row_index, 1, keepdims=False).astype(
            jnp.float32
        )
        product_row = pert_row * piece_rows[row_offset][None]
        current = lax.dynamic_index_in_dim(running, slot_index, 1, keepdims=False)
        running = lax.dynamic_update_index_in_dim(running, current + product_row, slot_index, 1)
    increment = settle(running, perturbations, counts, own_rows, norm_scale)
    return increment


def solution(mesh):
    return jax.shard_map(
        per_device,
        mesh=mesh,
        in_specs=(P("mem", "strip", None), P("mem", None, "strip", None), P("strip", None)),
        out_specs=P("mem", "strip", None),
        check_vma=False,
    )
```

profile of v0, /device:TPU:7, one launch (start us, length us, event | category | flops | bytes accessed | tf_op | source)
XLA Modules:
  0.0 118.1 jit_solution(14257599412685064002)
XLA Ops:
  0.0 2.1 %broadcast_in_dim.17 = f32[4,2,32,1024]{3,2,1,0:T(8,128)} broadcast(f32[2,32,1024]{2,1,0:T(8,128)} %param.3), dimensions={1,2,3} | broadcast | bytes 1310720 | tf_op jit(solution)/shard_map/broadcast_in_dim | solution.py:49
  2.1 5.1 %all-to-all-start = ((f32[4,2,32,1024]{3,2,1,0:T(8,128)}), f32[4,2,32,1024]{3,2,1,0:T(8,128)}, u32[]{:S(2)}, u32[]{:S(2)}) async-start(f32[4,2,32,1024]{3,2,1,0:T(8,128)} %broadcast_in_dim.17), calls=%async_computation | async-start | bytes 2097152 | tf_op jit(solution)/shard_map/all_to_all | solution.py:50
  7.2 5.8 %fusion.46 = (bf16[16,1,32,1024]{3,2,1,0:T(8,128)(2,1)S(1)}, bf16[16,1,32,1024]{3,2,1,0:T(8,128)(2,1)}, bf16[16,1,32,1024]{3,2,1,0:T(8,128)(2,1)}, bf16[16,1,32,...) fusion(bf16[16,8,32,1024]{3,2,1,0:T(8,128)(2,1)} %param.4), kind=kLoop, calls=%fused_computation.92 | loop fusion | bytes 16777216 | tf_op jit(solution)/shard_map/jit(dynamic_index_in_dim)/dynamic_slice | solution.py:106
  13.0 9.3 %all-to-all-done = f32[4,2,32,1024]{3,2,1,0:T(8,128)} async-done(((f32[4,2,32,1024]{3,2,1,0:T(8,128)}), f32[4,2,32,1024]{3,2,1,0:T(8,128)}, u32[]{:S(2)}, u32[]{:S(2)}) %all-to-all-start) | async-done | bytes 1048608 | tf_op jit(solution)/shard_map/all_to_all | solution.py:50
  22.3 1.4 %slice_bitcast_fusion = (f32[32,1024]{1,0:T(8,128)S(1)}, f32[32,1024]{1,0:T(8,128)S(1)}, f32[32,1024]{1,0:T(8,128)S(1)}, f32[32,1024]{1,0:T(8,128)S(1)}, f32[32,...) fusion(f32[8,32,1024]{2,1,0:T(8,128)} %bitcast), kind=kLoop, calls=%fused_computation.75 | loop fusion | bytes 2097152 | tf_op jit(solution)/shard_map/mul | solution.py:109
  23.6 0.7 convert_multiply_fusion.15
  24.3 0.0 copy-start.4
  24.3 0.6 dynamic_update_slice.25
  24.9 0.0 copy-start.9
  24.9 1.4 %fusion.44 = f32[16,2,32,1024]{3,0,2,1:T(8,128)S(1)} fusion(f32[16,2,32,1024]{3,0,2,1:T(8,128)S(1)} %dynamic_update_slice.25, f32[32,1024]{1,0:T(8,128)S(1)} %get-tuple-element.31, bf16[16,1,32,1024]{3,2,1,0:T(8,128)(2,1)S(1)} %get-tuple-element.21, f32[32,1024]{1,0:T(8,128)S(1)} %get-tuple-element.32, bf16[16,1,32,1024]{3,2,1,0:T(8,128)(2,1)S(1)} %get-tuple-element.22), kind=kLoop, calls=%fused_computation.69 | loop fusion | flops 2621440 | bytes 4456448 | tf_op jit(solution)/shard_map/jit(dynamic_update_index_in_dim)/dynamic_update_slice | solution.py:111
  26.4 2.1 %fusion.42 = f32[16,2,32,1024]{3,0,2,1:T(8,128)S(1)} fusion(f32[16,2,32,1024]{3,0,2,1:T(8,128)S(1)} %fusion.44, f32[32,1024]{1,0:T(8,128)S(1)} %get-tuple-element.30, bf16[16,1,32,1024]{3,2,1,0:T(8,128)(2,1)S(1)} %copy-done.4, f32[32,1024]{1,0:T(8,128)S(1)} %get-tuple-element.31, bf16[16,1,32,1024]{3,2,1,0:T(8,128)(2,1)S(1)} %get-tuple-element.21, ...), kind=kLoop, calls=%fused_computation.67 | loop fusion | flops 4194304 | bytes 5636096 | tf_op jit(solution)/shard_map/jit(dynamic_update_index_in_dim)/dynamic_update_slice | solution.py:111
  28.5 2.8 %fusion.30 = f32[16,2,32,1024]{3,0,2,1:T(8,128)S(1)} fusion(f32[16,2,32,1024]{3,0,2,1:T(8,128)S(1)} %fusion.42, f32[32,1024]{1,0:T(8,128)S(1)} %get-tuple-element.29, f32[32,1024]{1,0:T(8,128)S(1)} %get-tuple-element.30, bf16[16,1,32,1024]{3,2,1,0:T(8,128)(2,1)S(1)} %copy-done.9, bf16[16,1,32,1024]{3,2,1,0:T(8,128)(2,1)S(1)} %copy-done.4, ...), kind=kLoop, calls=%fused_computation.55 | loop fusion | flops 5767168 | bytes 6815744 | tf_op jit(solution)/shard_map/jit(dynamic_update_index_in_dim)/dynamic_update_slice | solution.py:111
  31.3 0.0 copy-start.2
  31.3 0.6 copy.66
  31.9 0.6 copy-done.2
  32.5 1.1 fusion.43
  33.6 1.5 %constant_dynamic-update-slice_fusion = (f32[16,2,32,1024]{3,0,2,1:T(8,128)S(1)}, f32[16,1,32,1024]{3,0,2,1:T(8,128)S(1)}) fusion(f32[16,2,32,1024]{3,0,2,1:T(8,128)S(1)} %fusion.43, f32[32,1024]{1,0:T(8,128)S(1)} %get-tuple-element.27, bf16[16,1,32,1024]{3,2,1,0:T(8,128)(2,1)S(1)} %copy-done.8, f32[32,1024]{1,0:T(8,128)S(1)} %get-tuple-element.28, ...), kind=kLoop, calls=%fused_computation.91 | loop fusion | flops 3145728 | bytes 8650752 | tf_op jit(solution)/shard_map/jit(dynamic_update_index_in_dim)/dynamic_update_slice | solution.py:111
  35.1 0.8 fusion.41
  35.9 0.0 copy-start.13
  35.9 1.7 %fusion.39 = f32[16,2,32,1024]{3,0,2,1:T(8,128)S(1)} fusion(f32[16,2,32,1024]{3,0,2,1:T(8,128)S(1)} %fusion.41, f32[16,1,32,1024]{3,0,2,1:T(8,128)S(1)} %get-tuple-element.14, f32[32,1024]{1,0:T(8,128)S(1)} %get-tuple-element.25, f32[32,1024]{1,0:T(8,128)S(1)} %get-tuple-element.26, bf16[16,1,32,1024]{3,2,1,0:T(8,128)(2,1)S(1)} %get-tuple-element.15, ...), kind=kLoop, calls=%fused_computation.64 | loop fusion | flops 3145728 | bytes 6553600 | tf_op jit(solution)/shard_map/jit(dynamic_update_index_in_dim)/dynamic_update_slice | solution.py:111
  37.7 0.1 fusion.47
  37.8 3.5 %collective-permute-start = (f32[16,2,4,1024]{3,0,2,1:T(8,128)S(1)}, f32[16,2,4,1024]{3,0,2,1:T(8,128)S(1)}, u32[]{:S(2)}, u32[]{:S(2)}) collective-permute-start(f32[16,2,4,1024]{3,0,2,1:T(8,128)S(1)} %get-tuple-element.23), channel_id=1, source_target_pairs={{0,1},{1,2},{2,3},{3,4},{4,5},{5,6},{6,7},{7,8},{8,9},{9,10},{10,1... | collective-permute-start | bytes 1572872 | tf_op jit(solution)/shard_map/ppermute | solution.py:25
  41.3 6.9 %collective-permute-start.1 = (f32[16,2,4,1024]{3,0,2,1:T(8,128)S(1)}, f32[16,2,4,1024]{3,0,2,1:T(8,128)S(1)}, u32[]{:S(2)}, u32[]{:S(2)}) collective-permute-start(f32[16,2,4,1024]{3,0,2,1:T(8,128)S(1)} %get-tuple-element.24), channel_id=1, source_target_pairs={{1,0},{2,1},{3,2},{4,3},{5,4},{6,5},{7,6},{8,7},{9,8},{10,9},{11,1... | collective-permute-start | bytes 1572872 | tf_op jit(solution)/shard_map/ppermute | solution.py:26
  48.2 0.0 copy-done.13
  48.3 1.9 %collective-permute-start.2 = (s32[4,1024]{1,0:T(4,128)S(1)}, s32[4,1024]{1,0:T(4,128)S(1)}, u32[]{:S(2)}, u32[]{:S(2)}) collective-permute-start(s32[4,1024]{1,0:T(4,128)S(1)} %get-tuple-element.37), channel_id=1, source_target_pairs={{0,1},{1,2},{2,3},{3,4},{4,5},{5,6},{6,7},{7,8},{8,9},{9,10},{10,1... | collective-permute-start | bytes 49160 | tf_op jit(solution)/shard_map/ppermute | solution.py:25
  50.2 6.4 %collective-permute-start.3 = (s32[4,1024]{1,0:T(4,128)S(1)}, s32[4,1024]{1,0:T(4,128)S(1)}, u32[]{:S(2)}, u32[]{:S(2)}) collective-permute-start(s32[4,1024]{1,0:T(4,128)S(1)} %get-tuple-element.38), channel_id=1, source_target_pairs={{1,0},{2,1},{3,2},{4,3},{5,4},{6,5},{7,6},{8,7},{9,8},{10,9},{11,1... | collective-permute-start | bytes 49160 | tf_op jit(solution)/shard_map/ppermute | solution.py:26
  56.6 1.4 %collective-permute-done.2 = s32[4,1024]{1,0:T(4,128)S(1)} collective-permute-done((s32[4,1024]{1,0:T(4,128)S(1)}, s32[4,1024]{1,0:T(4,128)S(1)}, u32[]{:S(2)}, u32[]{:S(2)}) %collective-permute-start.2) | collective-permute-done | bytes 16416 | tf_op jit(solution)/shard_map/ppermute | solution.py:25
  58.0 0.9 collective-permute-done.3
  58.9 0.8 compare_convert_fusion
  59.7 0.0 collective-permute-done
  59.7 0.0 collective-permute-done.1
  59.7 0.8 copy-done.10
  60.5 0.8 pad_maximum_fusion
  61.3 0.9 pad.27
  62.2 5.5 %fusion.5 = f32[16,2,40,1024]{3,0,2,1:T(8,128)S(1)} fusion(f32[16,2,42,1024]{3,0,2,1:T(8,128)S(1)} %pad.27, f32[40,1024]{1,0:T(8,128)} %get-tuple-element.36, f32[16,2,4,1024]{3,0,2,1:T(8,128)} %copy-done.10, f32[16,2,32,1024]{3,0,2,1:T(8,128)S(1)} %fusion.39, f32[16,2,4,1024]{3,0,2,1:T(8,128)S(1)} %collective-permute-done), kind=kLoop, calls=%fused_computation.13 | loop fusion | flops 15728640 | bytes 26640384 | tf_op jit(solution)/shard_map/add | solution.py:62
  67.7 0.0 copy-start.12
  67.7 0.5 pad.29
  68.1 0.4 copy-done.12
  68.6 3.9 %fusion.11 = f32[16,2,40,1024]{3,0,2,1:T(8,128)S(1)} fusion(f32[16,2,40,1024]{3,0,2,1:T(8,128)S(1)} %fusion.5, f32[16,2,42,1024]{3,0,2,1:T(8,128)S(1)} %pad.29, f32[40,1024]{1,0:T(8,128)S(1)} %copy-done.12), kind=kLoop, calls=%fused_computation.19 | loop fusion | flops 13107200 | bytes 26640384 | tf_op jit(solution)/shard_map/add | solution.py:62
  72.4 0.0 copy-start.11
  72.5 0.5 pad.31
  72.9 0.4 copy-done.11
  73.4 3.9 %fusion.17 = f32[16,2,40,1024]{3,0,2,1:T(8,128)S(1)} fusion(f32[16,2,40,1024]{3,0,2,1:T(8,128)S(1)} %fusion.11, f32[16,2,42,1024]{3,0,2,1:T(8,128)S(1)} %pad.31, f32[40,1024]{1,0:T(8,128)S(1)} %copy-done.11), kind=kLoop, calls=%fused_computation.25 | loop fusion | flops 13107200 | bytes 26640384 | tf_op jit(solution)/shard_map/add | solution.py:62
  77.2 0.9 pad.33
  78.1 4.0 %fusion.23 = f32[16,2,40,1024]{3,0,2,1:T(8,128)S(1)} fusion(f32[16,2,40,1024]{3,0,2,1:T(8,128)S(1)} %fusion.17, f32[16,2,42,1024]{3,0,2,1:T(8,128)S(1)} %pad.33, f32[40,1024]{1,0:T(8,128)S(1)} %get-tuple-element.33), kind=kLoop, calls=%fused_computation.31 | loop fusion | flops 13107200 | bytes 26640384 | tf_op jit(solution)/shard_map/add | solution.py:62
  82.2 15.8 %fusion.40 = (f32[32,1024]{1,0:T(8,128)S(1)}, f32[32,1024]{1,0:T(8,128)S(1)}, f32[32,1024]{1,0:T(8,128)S(1)}, f32[32,1024]{1,0:T(8,128)S(1)}, f32[32,1024]{1,0:T...) fusion(f32[16,2,40,1024]{3,0,2,1:T(8,128)S(1)} %fusion.23, ...), kind=kLoop, calls=%fused_computation.65 | loop fusion | flops 12320768 | bytes 13631488 | tf_op jit(solution)/shard_map/reduce_sum | solution.py:90
  98.2 19.1 %all_to_all.10 = f32[4,2,32,1024]{3,2,1,0:T(8,128)S(1)} all-to-all(f32[4,2,32,1024]{3,2,1,0:T(8,128)S(1)} %bitcast.34), channel_id=1, replica_groups=mesh['mem'=4,'strip'=64] {'mem'}, dimensions={0} | all-to-all | bytes 2097152 | tf_op jit(solution)/shard_map/all_to_all | solution.py:38
  117.3 0.8 reduce_sum.89
  (26 shorter events, 0.2 us)
Async XLA Ops:
  2.1 20.2 %all-to-all-start = ((f32[4,2,32,1024]{3,2,1,0:T(8,128)}), f32[4,2,32,1024]{3,2,1,0:T(8,128)}, u32[]{:S(2)}, u32[]{:S(2)}) async-start(f32[4,2,32,1024]{3,2,1,0:T(8,128)} %broadcast_in_dim.17), calls=%async_computation | async-start | bytes 2097152 | tf_op jit(solution)/shard_map/all_to_all | solution.py:50
  13.0 22.9 %copy-start.6 = (bf16[16,1,32,1024]{3,2,1,0:T(8,128)(2,1)}, bf16[16,1,32,1024]{3,2,1,0:T(8,128)(2,1)S(1)}, u32[]{:S(2)}) copy-start(bf16[16,1,32,1024]{3,2,1,0:T(8,128)(2,1)S(1)} %get-tuple-element.15) | copy-start | bytes 3145732
  24.3 2.0 %copy-start.4 = (bf16[16,1,32,1024]{3,2,1,0:T(8,128)(2,1)S(1)}, bf16[16,1,32,1024]{3,2,1,0:T(8,128)(2,1)}, u32[]{:S(2)}) copy-start(bf16[16,1,32,1024]{3,2,1,0:T(8,128)(2,1)} %get-tuple-element.20) | copy-start | bytes 3145732
  24.9 3.5 %copy-start.9 = (bf16[16,1,32,1024]{3,2,1,0:T(8,128)(2,1)S(1)}, bf16[16,1,32,1024]{3,2,1,0:T(8,128)(2,1)}, u32[]{:S(2)}) copy-start(bf16[16,1,32,1024]{3,2,1,0:T(8,128)(2,1)} %get-tuple-element.19) | copy-start | bytes 3145732
  31.3 1.2 %copy-start.2 = (bf16[16,1,32,1024]{3,2,1,0:T(8,128)(2,1)S(1)}, bf16[16,1,32,1024]{3,2,1,0:T(8,128)(2,1)}, u32[]{:S(2)}) copy-start(bf16[16,1,32,1024]{3,2,1,0:T(8,128)(2,1)} %get-tuple-element.18) | copy-start | bytes 3145732
  31.8 1.7 %copy-start.8 = (bf16[16,1,32,1024]{3,2,1,0:T(8,128)(2,1)S(1)}, bf16[16,1,32,1024]{3,2,1,0:T(8,128)(2,1)}, u32[]{:S(2)}) copy-start(bf16[16,1,32,1024]{3,2,1,0:T(8,128)(2,1)} %get-tuple-element.17) | copy-start | bytes 3145732
  33.6 1.6 %copy-start = (bf16[16,1,32,1024]{3,2,1,0:T(8,128)(2,1)S(1)}, bf16[16,1,32,1024]{3,2,1,0:T(8,128)(2,1)}, u32[]{:S(2)}) copy-start(bf16[16,1,32,1024]{3,2,1,0:T(8,128)(2,1)} %get-tuple-element.16) | copy-start | bytes 3145732
  35.9 12.3 %copy-start.13 = (s32[32,1024]{1,0:T(8,128)S(1)}, s32[32,1024]{1,0:T(8,128)}, u32[]{:S(2)}) copy-start(s32[32,1024]{1,0:T(8,128)} %param.5) | copy-start | bytes 393220
  37.8 21.9 %collective-permute-start = (f32[16,2,4,1024]{3,0,2,1:T(8,128)S(1)}, f32[16,2,4,1024]{3,0,2,1:T(8,128)S(1)}, u32[]{:S(2)}, u32[]{:S(2)}) collective-permute-start(f32[16,2,4,1024]{3,0,2,1:T(8,128)S(1)} %get-tuple-element.23), channel_id=1, source_target_pairs={{0,1},{1,2},{2,3},{3,4},{4,5},{5,6},{6,7},{7,8},{8,9},{9,10},{10,1... | collective-permute-start | bytes 1572872 | tf_op jit(solution)/shard_map/ppermute | solution.py:25
  41.3 18.3 %collective-permute-start.1 = (f32[16,2,4,1024]{3,0,2,1:T(8,128)S(1)}, f32[16,2,4,1024]{3,0,2,1:T(8,128)S(1)}, u32[]{:S(2)}, u32[]{:S(2)}) collective-permute-start(f32[16,2,4,1024]{3,0,2,1:T(8,128)S(1)} %get-tuple-element.24), channel_id=1, source_target_pairs={{1,0},{2,1},{3,2},{4,3},{5,4},{6,5},{7,6},{8,7},{9,8},{10,9},{11,1... | collective-permute-start | bytes 1572872 | tf_op jit(solution)/shard_map/ppermute | solution.py:26
  48.3 9.7 %collective-permute-start.2 = (s32[4,1024]{1,0:T(4,128)S(1)}, s32[4,1024]{1,0:T(4,128)S(1)}, u32[]{:S(2)}, u32[]{:S(2)}) collective-permute-start(s32[4,1024]{1,0:T(4,128)S(1)} %get-tuple-element.37), channel_id=1, source_target_pairs={{0,1},{1,2},{2,3},{3,4},{4,5},{5,6},{6,7},{7,8},{8,9},{9,10},{10,1... | collective-permute-start | bytes 49160 | tf_op jit(solution)/shard_map/ppermute | solution.py:25
  50.2 8.7 %collective-permute-start.3 = (s32[4,1024]{1,0:T(4,128)S(1)}, s32[4,1024]{1,0:T(4,128)S(1)}, u32[]{:S(2)}, u32[]{:S(2)}) collective-permute-start(s32[4,1024]{1,0:T(4,128)S(1)} %get-tuple-element.38), channel_id=1, source_target_pairs={{1,0},{2,1},{3,2},{4,3},{5,4},{6,5},{7,6},{8,7},{9,8},{10,9},{11,1... | collective-permute-start | bytes 49160 | tf_op jit(solution)/shard_map/ppermute | solution.py:26
  59.7 0.8 copy-start.10
  67.7 0.9 copy-start.12
  72.4 0.9 copy-start.11
  78.1 4.0 %copy-start.1 = (bf16[16,1,32,1024]{3,2,1,0:T(8,128)(2,1)S(1)}, bf16[16,1,32,1024]{3,2,1,0:T(8,128)(2,1)}, u32[]{:S(2)}) copy-start(bf16[16,1,32,1024]{3,2,1,0:T(8,128)(2,1)} %get-tuple-element.16) | copy-start | bytes 3145732
  78.1 4.0 %copy-start.3 = (bf16[16,1,32,1024]{3,2,1,0:T(8,128)(2,1)S(1)}, bf16[16,1,32,1024]{3,2,1,0:T(8,128)(2,1)}, u32[]{:S(2)}) copy-start(bf16[16,1,32,1024]{3,2,1,0:T(8,128)(2,1)} %get-tuple-element.18) | copy-start | bytes 3145732
  78.1 4.0 %copy-start.5 = (bf16[16,1,32,1024]{3,2,1,0:T(8,128)(2,1)S(1)}, bf16[16,1,32,1024]{3,2,1,0:T(8,128)(2,1)}, u32[]{:S(2)}) copy-start(bf16[16,1,32,1024]{3,2,1,0:T(8,128)(2,1)} %get-tuple-element.20) | copy-start | bytes 3145732
  78.1 4.0 %copy-start.7 = (bf16[16,1,32,1024]{3,2,1,0:T(8,128)(2,1)S(1)}, bf16[16,1,32,1024]{3,2,1,0:T(8,128)(2,1)}, u32[]{:S(2)}) copy-start(bf16[16,1,32,1024]{3,2,1,0:T(8,128)(2,1)} %copy-done.6) | copy-start | bytes 3145732
where the time goes:
time: 119 us; the launch traced here: 118 us
  other arithmetic  47.6 us (40%)
  starting transfers between devices  23.9 us (20%)
  blocking collectives  19.1 us (16%)
  local copies, waits for them, and re-layouts  15.5 us (13%)
  waiting for transfers between devices  11.6 us (10%)
    all_to_all x1, blocking collectives, sent_and_summed(): lax.all_to_all(blocks, axis, split_axis=0, concat_axis=0, tiled=True)  19.1 us
    add x4, other arithmetic, advance(): return centre + active * (COEFF_X * along_x + COEFF_Y * along_y)  17.1 us
    reduce_sum x1, other arithmetic, settle(): results.append(jnp.sum(pert_row * chosen, axis=0) * norm_scale)  15.8 us
    ppermute x2, starting transfers between devices, with_halo(): after = lax.ppermute(initial, axis, down)  13.3 us
    dynamic_update_slice x7, other arithmetic, per_device(): lax.dynamic_update_index_in_dim(running, current + product_row, slot_inde...  11.4 us
    all_to_all x1, waiting for transfers between devices, copy_for_each(): return lax.all_to_all(copies, axis, split_axis=0, concat_axis=0, tiled=True)  9.28 us
    dynamic_slice x1, local copies, waits for them, and re-layouts, per_device(): lax.dynamic_index_in_dim(perturbations, row_index, 1, keepdims=False)  5.79 us
    ppermute x2, starting transfers between devices, with_halo(): before = lax.ppermute(last, axis, up)  5.47 us
  transfers between devices with their start and end apart: 5, of which 3 were waited for; matrix products, arithmetic and copies ran while one was open for 6% of the time, Pallas kernels for 0%

commit v1 on v0

v1 whole, which is shorter than its diff:
```python
import math

import jax
import jax.numpy as jnp
from jax import lax
from jax.experimental import pallas as pl
from jax.experimental.pallas import tpu as pltpu
from jax.sharding import PartitionSpec as P

MESH = pl.DeviceIdType.MESH
SLOTS, VARS, FIELDS, SWEEPS = 2, 4, 8, 4
CX, NY, K = 32, 1024, 16
LANES = 128
CB = NY // LANES
HALO = SWEEPS
UNROLL = 2
KX, KY = 0.35, 0.12
ALPHA = KY / KX
GAMMA = (1.0 - 2.0 * KX - 2.0 * KY) / KX
BETA = 2.0 + 2.0 * ALPHA
PITCH = 9
PIECES = ((0, 8), (24, 8), (8, 16))


def remote(src, dst, send, recv, device):
    return pltpu.make_async_remote_copy(
        src_ref=src, dst_ref=dst, send_sem=send, recv_sem=recv, device_id=device, device_id_type=MESH
    )


def lanes_of(cb):
    return pl.ds(pl.multiple_of(cb * LANES, LANES), LANES)


def kernel(
    norm, strips,
    grad, pert, counts, own_ref, other_ref,
    pv, gv, cv, ct, cn, u, near, sent, edge, coef, inc, part, csum, osum,
    pert_sem, load_sem, gsend, grecv, csend, crecv, hsend, hrecv, psend, precv, rsend, rrecv, out_sem,
):
    m, s = lax.axis_index("mem"), lax.axis_index("strip")
    chip, core = lax.div(m, 2), lax.rem(m, 2)
    m1, m2 = m + 1 - 2 * core, lax.rem(m + 2, 4)
    m3 = m2 + 1 - 2 * core
    mine, theirs = chip, 1 - chip
    has_up, has_down = s > 0, s < strips - 1
    slots = (mine, theirs)

    loads = []
    for i, (first, size) in enumerate(PIECES):
        for j, sl in enumerate(slots):
            fields, rows = pl.ds(sl * VARS, VARS), pl.ds(first, size)
            loads.append(pltpu.make_async_copy(
                pert.at[:, fields, rows, :], pv.at[:, fields, rows, :], pert_sem.at[j, i]))
    load_g = pltpu.make_async_copy(grad, gv.at[m], load_sem.at[0])
    load_c = pltpu.make_async_copy(counts, cv, load_sem.at[1])
    load_g.start()
    load_c.start()
    for copy in loads:
        copy.start()

    barrier = pltpu.get_barrier_semaphore()
    for device in ((m1, s), (m2, s)):
        pl.semaphore_signal(barrier, inc=1, device_id=device, device_id_type=MESH)

    @pl.when(has_up)
    def _():
        pl.semaphore_signal(barrier, inc=1, device_id=(m, s - 1), device_id_type=MESH)

    @pl.when(has_down)
    def _():
        pl.semaphore_signal(barrier, inc=1, device_id=(m, s + 1), device_id_type=MESH)

    pl.semaphore_wait(barrier, 2 + has_up.astype(jnp.int32) + has_down.astype(jnp.int32))

    to_core, to_chip, onward = [], [], []
    for i, (first, size) in enumerate(PIECES):
        rows = pl.ds(first, size)
        to_core.append(remote(grad.at[:, rows, :], gv.at[m, :, rows, :], gsend.at[0, i], grecv.at[0, i], (m1, s)))
        to_chip.append(remote(grad.at[:, rows, :], gv.at[m, :, rows, :], gsend.at[1, i], grecv.at[1, i], (m2, s)))
        onward.append(remote(
            gv.at[m2, :, rows, :], gv.at[m2, :, rows, :], gsend.at[2, i], grecv.at[2, i], (m1, s)))
    c_up = remote(counts.at[pl.ds(0, 8), :], cn, csend.at[0], crecv.at[0], (m, s - 1))
    c_down = remote(counts.at[pl.ds(24, 8), :], ct, csend.at[1], crecv.at[1], (m, s + 1))

    def halos(sl):
        up = remote(sent.at[sl, 0], near.at[sl, 1],
                    hsend.at[sl, 0], hrecv.at[sl, 0], (m, s - 1))
        down = remote(sent.at[sl, 1], near.at[sl, 0],
                      hsend.at[sl, 1], hrecv.at[sl, 1], (m, s + 1))
        return up, down

    def start_both(up, down):
        @pl.when(has_up)
        def _():
            up.start()

        @pl.when(has_down)
        def _():
            down.start()

    def wait_recv_both(up, down):
        @pl.when(has_down)
        def _():
            up.wait_recv()

        @pl.when(has_up)
        def _():
            down.wait_recv()

    def wait_send_both(up, down):
        @pl.when(has_up)
        def _():
            up.wait_send()

        @pl.when(has_down)
        def _():
            down.wait_send()

    start_both(c_up, c_down)
    for i in range(2):
        to_chip[i].start()
        to_core[i].start()

    def project(sl, pieces):
        def column(cb, carry):
            lanes = lanes_of(cb)
            for first, size in pieces:
                rows = pl.ds(first, size)
                g = [gv[2 * sl + v // 2, v % 2, rows, lanes] for v in range(VARS)]
                for k in range(K):
                    total = pv[k, sl * VARS, rows, lanes].astype(jnp.float32) * g[0]
                    for v in range(1, VARS):
                        total = total + pv[k, sl * VARS + v, rows, lanes].astype(jnp.float32) * g[v]
                    for i in range(0, size, 8):
                        u[sl, k // 8, cb, pl.ds((first + i) * PITCH + k % 8, 8, stride=PITCH), :] = total[i : i + 8]
            for side, x0 in ((0, 0), (1, CX - HALO)):
                if any(first <= x0 < first + size for first, size in pieces):
                    for i in range(HALO):
                        for h in range(2):
                            sent[sl, side, h, cb, i] = u[sl, h, cb, pl.ds((x0 + i) * PITCH, 8), :]
            return carry

        lax.fori_loop(0, CB, column, 0, unroll=UNROLL)

    def zero_outside(sl):
        @pl.when(jnp.logical_not(has_up))
        def _():
            near[sl, 0] = jnp.zeros(near.shape[2:], jnp.float32)

        @pl.when(jnp.logical_not(has_down))
        def _():
            near[sl, 1] = jnp.zeros(near.shape[2:], jnp.float32)

    lane = lax.broadcasted_iota(jnp.int32, (8, LANES), 1)
    at_first, at_last = lane == 0, lane == LANES - 1
    zero = jnp.zeros((8, LANES), jnp.float32)
    on_grid = [jnp.where(has, jnp.ones((8, LANES), jnp.float32), 0.0) for has in (has_up, has_down)]

    def row_of(sl, x, h):
        if x < 0:
            return [near[sl, 0, h, cb, HALO + x] for cb in range(CB)]
        if x >= CX:
            return [near[sl, 1, h, cb, x - CX] for cb in range(CB)]
        return [u[sl, h, cb, pl.ds(x * PITCH, 8), :] for cb in range(CB)]

    def put_row(sl, x, h, values):
        for cb in range(CB):
            if x < 0:
                near[sl, 0, h, cb, HALO + x] = values[cb]
            elif x >= CX:
                near[sl, 1, h, cb, x - CX] = values[cb]
            else:
                u[sl, h, cb, pl.ds(x * PITCH, 8), :] = values[cb]

    def advanced(before, centre, after, t, x):
        right = [pltpu.roll(c, 1, 1) for c in centre]
        left = [pltpu.roll(c, LANES - 1, 1) for c in centre]
        out = []
        for cb in range(CB):
            low = jnp.where(at_first, right[cb - 1] if cb > 0 else zero, right[cb])
            high = jnp.where(at_last, left[cb + 1] if cb < CB - 1 else zero, left[cb])
            total = (before[cb] + after[cb]) + ALPHA * (low + high)
            if t == 0:
                total = total + GAMMA * centre[cb]
                out.append(total if 0 <= x < CX else on_grid[x >= CX] * total)
            else:
                out.append(centre[cb] + coef[t - 1, cb, HALO + x] * (total - BETA * centre[cb]))
        return out

    def inner_sweeps(sl, halves):
        def half(h, carry):
            for t in range(SWEEPS):
                first, last = t + 1, CX - 2 - t
                before, centre = row_of(sl, first - 1, h), row_of(sl, first, h)
                for cb in range(CB):
                    edge[sl, 0, t, h, cb] = centre[cb]
                for x in range(first, last + 1):
                    after = row_of(sl, x + 1, h)
                    if x == last:
                        for cb in range(CB):
                            edge[sl, 1, t, h, cb] = centre[cb]
                    put_row(sl, x, h, advanced(before, centre, after, t, x))
                    before, centre = centre, after
            return carry

        lax.fori_loop(*halves, half, 0)

    def outer_sweeps(sl):
        def half(h, carry):
            for t in range(SWEEPS):
                before, centre = row_of(sl, t - HALO, h), row_of(sl, t - HALO + 1, h)
                for x in range(t - HALO + 1, t + 1):
                    after = [edge[sl, 0, t, h, cb] for cb in range(CB)] if x == t else row_of(sl, x + 1, h)
                    put_row(sl, x, h, advanced(before, centre, after, t, x))
                    before, centre = centre, after
                before, centre = [edge[sl, 1, t, h, cb] for cb in range(CB)], row_of(sl, CX - 1 - t, h)
                for x in range(CX - 1 - t, CX + HALO - 1 - t):
                    after = row_of(sl, x + 1, h)
                    put_row(sl, x, h, advanced(before, centre, after, t, x))
                    before, centre = centre, after
            return carry

        lax.fori_loop(0, 2, half, 0)

    def increments(sl, pieces):
        def column(cb, carry):
            lanes = lanes_of(cb)
            for first, size in pieces:
                for x in range(first, first + size, 8):
                    rows = pl.ds(x, 8)
                    total = [None] * VARS
                    for k in range(K):
                        smooth = u[sl, k // 8, cb, pl.ds(x * PITCH + k % 8, 8, stride=PITCH), :]
                        for v in range(VARS):
                            term = pv[k, sl * VARS + v, rows, lanes].astype(jnp.float32) * smooth
                            total[v] = term if k == 0 else total[v] + term
                    for v in range(VARS):
                        inc[sl, v // 2, v % 2, rows, lanes] = total[v] * (norm * KX)
            return carry

        lax.fori_loop(0, CB, column, 0, unroll=UNROLL)

    def to_partner(sl, i):
        rows = pl.ds(*PIECES[i])
        return remote(inc.at[sl, 1 - core, :, rows, :], part.at[sl, :, rows, :],
                      psend.at[sl, i], precv.at[sl, i], (m1, s))

    def to_owner(i):
        rows = pl.ds(*PIECES[i])
        return remote(csum.at[:, rows, :], other_ref.at[:, rows, :], rsend.at[i], rrecv.at[i], (m2, s))

    def out_copy(i):
        rows = pl.ds(*PIECES[i])
        return pltpu.make_async_copy(osum.at[:, rows, :], own_ref.at[:, rows, :], out_sem.at[i])

    def join(sl, i, into):
        first, size = PIECES[i]

        def column(cb, carry):
            lanes = lanes_of(cb)
            for v in range(2):
                rows = pl.ds(first, size)
                into[v, rows, lanes] = inc[sl, core, v, rows, lanes] + part[sl, v, rows, lanes]
            return carry

        lax.fori_loop(0, CB, column, 0)

    def wait_pert(j, i):
        fields, rows = pl.ds(slots[j] * VARS, VARS), pl.ds(*PIECES[i])
        pltpu.make_async_copy(
            pert.at[:, fields, rows, :], pv.at[:, fields, rows, :], pert_sem.at[j, i]).wait()

    edges, inner = PIECES[:2], PIECES[2:]
    load_g.wait()
    for i in range(2):
        wait_pert(0, i)
        to_core[i].wait_recv()
    project(mine, edges)
    start_both(*halos(mine))
    to_core[2].start()
    to_chip[2].start()

    load_c.wait()

    @pl.when(jnp.logical_not(has_up))
    def _():
        ct[...] = jnp.zeros(ct.shape, jnp.int32)

    @pl.when(jnp.logical_not(has_down))
    def _():
        cn[...] = jnp.zeros(cn.shape, jnp.int32)

    wait_recv_both(c_up, c_down)

    def weights(cb, carry):
        lanes = lanes_of(cb)
        for i in range(CX + 2 * HALO):
            x = i - HALO
            source, row = (ct, 8 + x) if x < 0 else (cn, x - CX) if x >= CX else (cv, x)
            c = jnp.broadcast_to(source[pl.ds(row, 1), lanes], (8, LANES))
            for t in range(1, SWEEPS):
                coef[t - 1, cb, i] = jnp.where(c > t, KX, 0.0)
        return carry

    lax.fori_loop(0, CB, weights, 0)

    zero_outside(mine)
    zero_outside(theirs)
    wait_pert(0, 2)
    to_core[2].wait_recv()
    project(mine, inner)
    inner_sweeps(mine, (0, 1))

    for i in range(2):
        to_chip[i].wait_recv()
        onward[i].start()
    for i in range(2):
        wait_pert(1, i)
        onward[i].wait_recv()
    project(theirs, edges)
    start_both(*halos(theirs))

    inner_sweeps(mine, (1, 2))
    to_chip[2].wait_recv()
    onward[2].start()
    increments(mine, inner)
    to_partner(mine, 2).start()

    wait_pert(1, 2)
    onward[2].wait_recv()
    project(theirs, inner)
    inner_sweeps(theirs, (0, 2))
    increments(theirs, inner)
    to_partner(theirs, 2).start()

    wait_recv_both(*halos(mine))
    outer_sweeps(mine)
    to_partner(theirs, 2).wait_recv()
    join(theirs, 2, csum)
    to_owner(2).start()
    increments(mine, edges)
    for i in range(2):
        to_partner(mine, i).start()

    wait_recv_both(*halos(theirs))
    outer_sweeps(theirs)
    increments(theirs, edges)
    for i in range(2):
        to_partner(theirs, i).start()
    for i in range(2):
        to_partner(theirs, i).wait_recv()
        join(theirs, i, csum)
        to_owner(i).start()

    for i in range(3):
        to_partner(mine, i).wait_recv()
        join(mine, i, osum)
        out_copy(i).start()
    for i in range(3):
        to_owner(i).wait_recv()
        out_copy(i).wait()

    for i in range(3):
        to_core[i].wait_send()
        to_chip[i].wait_send()
        onward[i].wait_send()
        to_owner(i).wait_send()
        for sl in slots:
            to_partner(sl, i).wait_send()
    wait_send_both(c_up, c_down)
    for sl in slots:
        wait_send_both(*halos(sl))


def per_device(gradient, perturbations, counts):
    members = perturbations.shape[0] * lax.axis_size("mem")
    strips = lax.axis_size("strip")
    norm = 1.0 / math.sqrt(members * FIELDS)
    own = gradient.shape
    dma = pltpu.SemaphoreType.DMA
    f32 = jnp.float32
    a, b = pl.pallas_call(
        lambda *refs: kernel(norm, strips, *refs),
        name="covariance",
        out_shape=[jax.ShapeDtypeStruct(own, f32)] * 2,
        in_specs=[pl.BlockSpec(memory_space=pltpu.HBM)] * 3,
        out_specs=[pl.BlockSpec(memory_space=pltpu.HBM)] * 2,
        scratch_shapes=[
            pltpu.VMEM(perturbations.shape, jnp.bfloat16),
            pltpu.VMEM((4, *own), f32),
            pltpu.VMEM(counts.shape, jnp.int32),
            pltpu.VMEM((8, NY), jnp.int32),
            pltpu.VMEM((8, NY), jnp.int32),
            pltpu.VMEM((SLOTS, 2, CB, CX * PITCH, LANES), f32),
            pltpu.VMEM((SLOTS, 2, 2, CB, HALO, 8, LANES), f32),
            pltpu.VMEM((SLOTS, 2, 2, CB, HALO, 8, LANES), f32),
            pltpu.VMEM((SLOTS, 2, SWEEPS, 2, CB, 8, LANES), f32),
            pltpu.VMEM((SWEEPS - 1, CB, CX + 2 * HALO, 8, LANES), f32),
            pltpu.VMEM((SLOTS, 2, 2, CX, NY), f32),
            pltpu.VMEM((SLOTS, 2, CX, NY), f32),
            pltpu.VMEM((2, CX, NY), f32),
            pltpu.VMEM((2, CX, NY), f32),
            dma((2, 3)), dma((2,)),
            dma((3, 3)), dma((3, 3)),
            dma((2,)), dma((2,)),
            dma((2, 2)), dma((2, 2)),
            dma((2, 3)), dma((2, 3)),
            dma((3,)), dma((3,)), dma((3,)),
        ],
        compiler_params=pltpu.CompilerParams(
            collective_id=0, has_side_effects=True, vmem_limit_bytes=58000 * 1024),
    )(gradient, perturbations, counts)
    return a + b


def solution(mesh):
    return jax.shard_map(
        per_device,
        mesh=mesh,
        in_specs=(P("mem", "strip", None), P("mem", None, "strip", None), P("strip", None)),
        out_specs=P("mem", "strip", None),
        check_vma=False,
    )
```

time: 119 us -> 47.8 us (0.40)
  Pallas kernels: 0 us -> 46 us
  other arithmetic: 47.6 us -> 1.76 us
  starting transfers between devices: 23.9 us -> 0 us
  blocking collectives: 19.1 us -> 0 us
  local copies, waits for them, and re-layouts: 15.5 us -> 0 us
  waiting for transfers between devices: 11.6 us -> 0 us
    pallas_call x0 -> x1, Pallas kernels: none -> 46 us  [per_device(): pl.pallas_call(lambda *refs: kernel(norm, strips, *refs), name='covarianc...]
    all_to_all x1 -> x0, blocking collectives: 19.1 us -> none  [sent_and_summed(): lax.all_to_all(blocks, axis, split_axis=0, concat_axis=0, tiled=True)]
    ppermute x4 -> x0, starting transfers between devices: 18.7 us -> none  [the longest x2 13.3 us: with_halo(): after = lax.ppermute(initial, axis, down)]
    reduce_sum x2 -> x0, other arithmetic: 16.6 us -> none  [the longest x1 15.8 us: settle(): results.append(jnp.sum(pert_row * chosen, axis=0) * norm_scale)]
    add x4 -> x1, other arithmetic: 17.1 us -> 1.76 us  [per_device(): return a + b]
    dynamic_update_slice x7 -> x0, other arithmetic: 11.4 us -> none  [per_device(): lax.dynamic_update_index_in_dim(running, current + product_row, slot_inde...]
    all_to_all x1 -> x0, waiting for transfers between devices: 9.28 us -> none  [copy_for_each(): return lax.all_to_all(copies, axis, split_axis=0, concat_axis=0, tiled=True)]
    dynamic_slice x1 -> x0, local copies, waits for them, and re-layouts: 5.79 us -> none  [per_device(): lax.dynamic_index_in_dim(perturbations, row_index, 1, keepdims=False)]
  transfers between devices with their start and end apart: 5 -> 0, of which waited for: 3 -> 0; matrix products, arithmetic and copies ran while one was open for 6% -> 0% of each run, Pallas kernels for 0% -> 0%
where the time goes in v1:
time: 47.8 us; the launch traced here: 47.7 us
  Pallas kernels  46 us (96%)
  other arithmetic  1.76 us (4%)
    pallas_call x1, Pallas kernels, per_device(): pl.pallas_call(lambda *refs: kernel(norm, strips, *refs), name='covarianc...  46 us
    add x1, other arithmetic, per_device(): return a + b  1.76 us

profile of v1, /device:TPU:7, one launch (start us, length us, event | category | flops | bytes accessed | tf_op | source)
XLA Modules:
  0.0 47.7 jit_solution(8504666020324584182)
XLA Ops:
  0.0 46.0 %covariance.1 = (f32[2,32,1024]{2,1,0:T(8,128)}, f32[2,32,1024]{2,1,0:T(8,128)}) custom-call(f32[2,32,1024]{2,1,0:T(8,128)} %refs_0_.1, bf16[16,8,32,1024]{3,2,1,0:T(8,128)(2,1)} %refs_1_.1, s32[32,1024]{1,0:T(8,128)} %refs_2_.1), custom_call_target="tpu_custom_call" | custom-call | tf_op jit(solution)/shard_map/covariance/pallas_call | solution.py:383
  46.0 1.8 %add.3 = f32[2,32,1024]{2,1,0:T(8,128)} add(f32[2,32,1024]{2,1,0:T(8,128)} %get-tuple-element.7, f32[2,32,1024]{2,1,0:T(8,128)} %get-tuple-element.8) | non-fusion elementwise | flops 65536 | bytes 786432 | tf_op jit(solution)/shard_map/add | solution.py:414

commit v2 on v1

--- a/solution.py
+++ b/solution.py
@@ -14,6 +14,7 @@
 CB = NY // LANES
 HALO = SWEEPS
 UNROLL = 2
+TURN = 8
 KX, KY = 0.35, 0.12
 ALPHA = KY / KX
 GAMMA = (1.0 - 2.0 * KX - 2.0 * KY) / KX
@@ -35,8 +36,8 @@
 def kernel(
     norm, strips,
     grad, pert, counts, own_ref, other_ref,
-    pv, gv, cv, ct, cn, u, near, sent, edge, coef, inc, part, csum, osum,
-    pert_sem, load_sem, gsend, grecv, csend, crecv, hsend, hrecv, psend, precv, rsend, rrecv, out_sem,
+    pv, gv, cv, ct, cn, u, near, sent, hop, edge, coef, inc, part, csum, osum,
+    pert_sem, load_sem, gsend, grecv, csend, crecv, hsend, hrecv, jsend, jrecv, psend, precv, rsend, rrecv, out_sem,
 ):
     m, s = lax.axis_index("mem"), lax.axis_index("strip")
     chip, core = lax.div(m, 2), lax.rem(m, 2)
@@ -45,6 +46,14 @@
     mine, theirs = chip, 1 - chip
     has_up, has_down = s > 0, s < strips - 1
     slots = (mine, theirs)
+    z = lax.rem(s, TURN)
+    turn_up, turn_down = jnp.logical_and(has_up, z == 0), jnp.logical_and(has_down, z == TURN - 1)
+    relay_down = jnp.logical_and(z == 1, s + TURN - 1 < strips)
+    relay_up = jnp.logical_and(z == TURN - 2, s >= TURN - 1)
+    roles = (
+        (turn_up, s + TURN - 2, s - TURN + 1), (turn_down, s - TURN + 2, s + TURN - 1),
+        (relay_down, s + TURN - 2, s + TURN - 1), (relay_up, s - TURN + 2, s - TURN + 1),
+    )
 
     loads = []
     for i, (first, size) in enumerate(PIECES):
@@ -71,7 +80,15 @@
     def _():
         pl.semaphore_signal(barrier, inc=1, device_id=(m, s + 1), device_id_type=MESH)
 
-    pl.semaphore_wait(barrier, 2 + has_up.astype(jnp.int32) + has_down.astype(jnp.int32))
+    expected = 2 + has_up.astype(jnp.int32) + has_down.astype(jnp.int32)
+    for role, *others in roles:
+        expected = expected + 2 * role.astype(jnp.int32)
+        for other in others:
+            @pl.when(role)
+            def _(other=other):
+                pl.semaphore_signal(barrier, inc=1, device_id=(m, other), device_id_type=MESH)
+
+    pl.semaphore_wait(barrier, expected)
 
     to_core, to_chip, onward = [], [], []
     for i, (first, size) in enumerate(PIECES):
@@ -83,12 +100,58 @@
     c_up = remote(counts.at[pl.ds(0, 8), :], cn, csend.at[0], crecv.at[0], (m, s - 1))
     c_down = remote(counts.at[pl.ds(24, 8), :], ct, csend.at[1], crecv.at[1], (m, s + 1))
 
-    def halos(sl):
-        up = remote(sent.at[sl, 0], near.at[sl, 1],
-                    hsend.at[sl, 0], hrecv.at[sl, 0], (m, s - 1))
-        down = remote(sent.at[sl, 1], near.at[sl, 0],
-                      hsend.at[sl, 1], hrecv.at[sl, 1], (m, s + 1))
-        return up, down
+    def halo(sl, side, h):
+        device = (m, s - 1 if side == 0 else s + 1)
+        return remote(sent.at[sl, side, h], near.at[sl, 1 - side, h], hsend.at[sl, side, h], hrecv.at[sl, side, h], device)
+
+    def to_relay(sl, side):
+        device = (m, s + TURN - 2 if side == 0 else s - TURN + 2)
+        return remote(sent.at[sl, side, 1], hop.at[sl], hsend.at[sl, side, 1], jrecv.at[sl], device)
+
+    def from_relay(sl, side):
+        device = (m, s - TURN + 1 if side == 0 else s + TURN - 1)
+        return remote(hop.at[sl], near.at[sl, 1 - side, 1], jsend.at[sl], hrecv.at[sl, side, 1], device)
+
+    sides = ((0, has_up, turn_up, relay_up), (1, has_down, turn_down, relay_down))
+
+    def send_halos(sl):
+        for side, has, turn, _ in sides:
+            @pl.when(has)
+            def _():
+                halo(sl, side, 0).start()
+
+            @pl.when(jnp.logical_and(has, jnp.logical_not(turn)))
+            def _():
+                halo(sl, side, 1).start()
+
+            @pl.when(turn)
+            def _():
+                to_relay(sl, side).start()
+
+    def pass_on(sl):
+        for side, _, _, relay in sides:
+            @pl.when(relay)
+            def _():
+                to_relay(sl, side).wait_recv()
+                from_relay(sl, side).start()
+
+    def wait_halos(sl):
+        for side, has in ((0, has_down), (1, has_up)):
+            @pl.when(has)
+            def _():
+                for h in range(2):
+                    halo(sl, side, h).wait_recv()
+
+    def end_halos(sl):
+        for side, has, _, relay in sides:
+            @pl.when(has)
+            def _():
+                for h in range(2):
+                    halo(sl, side, h).wait_send()
+
+            @pl.when(relay)
+            def _():
+                from_relay(sl, side).wait_send()
 
     def start_both(up, down):
         @pl.when(has_up)
@@ -277,36 +340,25 @@
         wait_pert(0, i)
         to_core[i].wait_recv()
     project(mine, edges)
-    start_both(*halos(mine))
+    send_halos(mine)
     to_core[2].start()
     to_chip[2].start()
 
     load_c.wait()
 
-    @pl.when(jnp.logical_not(has_up))
-    def _():
-        ct[...] = jnp.zeros(ct.shape, jnp.int32)
-
-    @pl.when(jnp.logical_not(has_down))
-    def _():
-        cn[...] = jnp.zeros(cn.shape, jnp.int32)
-
-    wait_recv_both(c_up, c_down)
-
-    def weights(cb, carry):
-        lanes = lanes_of(cb)
-        for i in range(CX + 2 * HALO):
-            x = i - HALO
-            source, row = (ct, 8 + x) if x < 0 else (cn, x - CX) if x >= CX else (cv, x)
-            c = jnp.broadcast_to(source[pl.ds(row, 1), lanes], (8, LANES))
-            for t in range(1, SWEEPS):
-                coef[t - 1, cb, i] = jnp.where(c > t, KX, 0.0)
-        return carry
-
-    lax.fori_loop(0, CB, weights, 0)
-
-    zero_outside(mine)
-    zero_outside(theirs)
+    def weights(rows):
+        def column(cb, carry):
+            lanes = lanes_of(cb)
+            for x in rows:
+                source, row = (ct, 8 + x) if x < 0 else (cn, x - CX) if x >= CX else (cv, x)
+                c = jnp.broadcast_to(source[pl.ds(row, 1), lanes], (8, LANES))
+                for t in range(1, SWEEPS):
+                    coef[t - 1, cb, HALO + x] = jnp.where(c > t, KX, 0.0)
+            return carry
+
+        lax.fori_loop(0, CB, column, 0)
+
+    weights(range(CX))
     wait_pert(0, 2)
     to_core[2].wait_recv()
     project(mine, inner)
@@ -319,31 +371,46 @@
         wait_pert(1, i)
         onward[i].wait_recv()
     project(theirs, edges)
-    start_both(*halos(theirs))
+    send_halos(theirs)
+    pass_on(mine)
 
     inner_sweeps(mine, (1, 2))
     to_chip[2].wait_recv()
     onward[2].start()
-    increments(mine, inner)
-    to_partner(mine, 2).start()
-
     wait_pert(1, 2)
     onward[2].wait_recv()
     project(theirs, inner)
-    inner_sweeps(theirs, (0, 2))
+    inner_sweeps(theirs, (0, 1))
+    pass_on(theirs)
+    inner_sweeps(theirs, (1, 2))
     increments(theirs, inner)
     to_partner(theirs, 2).start()
-
-    wait_recv_both(*halos(mine))
-    outer_sweeps(mine)
+    increments(mine, inner)
+    to_partner(mine, 2).start()
     to_partner(theirs, 2).wait_recv()
     join(theirs, 2, csum)
     to_owner(2).start()
+
+    zero_outside(mine)
+    zero_outside(theirs)
+
+    @pl.when(jnp.logical_not(has_up))
+    def _():
+        ct[...] = jnp.zeros(ct.shape, jnp.int32)
+
+    @pl.when(jnp.logical_not(has_down))
+    def _():
+        cn[...] = jnp.zeros(cn.shape, jnp.int32)
+
+    wait_recv_both(c_up, c_down)
+    weights([*range(-HALO, 0), *range(CX, CX + HALO)])
+    wait_halos(mine)
+    outer_sweeps(mine)
     increments(mine, edges)
     for i in range(2):
         to_partner(mine, i).start()
 
-    wait_recv_both(*halos(theirs))
+    wait_halos(theirs)
     outer_sweeps(theirs)
     increments(theirs, edges)
     for i in range(2):
@@ -370,7 +437,7 @@
             to_partner(sl, i).wait_send()
     wait_send_both(c_up, c_down)
     for sl in slots:
-        wait_send_both(*halos(sl))
+        end_halos(sl)
 
 
 def per_device(gradient, perturbations, counts):
@@ -395,6 +462,7 @@
             pltpu.VMEM((SLOTS, 2, CB, CX * PITCH, LANES), f32),
             pltpu.VMEM((SLOTS, 2, 2, CB, HALO, 8, LANES), f32),
             pltpu.VMEM((SLOTS, 2, 2, CB, HALO, 8, LANES), f32),
+            pltpu.VMEM((SLOTS, CB, HALO, 8, LANES), f32),
             pltpu.VMEM((SLOTS, 2, SWEEPS, 2, CB, 8, LANES), f32),
             pltpu.VMEM((SWEEPS - 1, CB, CX + 2 * HALO, 8, LANES), f32),
             pltpu.VMEM((SLOTS, 2, 2, CX, NY), f32),
@@ -404,7 +472,7 @@
             dma((2, 3)), dma((2,)),
             dma((3, 3)), dma((3, 3)),
             dma((2,)), dma((2,)),
-            dma((2, 2)), dma((2, 2)),
+            dma((2, 2, 2)), dma((2, 2, 2)), dma((2,)), dma((2,)),
             dma((2, 3)), dma((2, 3)),
             dma((3,)), dma((3,)), dma((3,)),
         ],

time: 47.8 us -> 43.8 us (0.916)
  Pallas kernels: 46 us -> 42 us
    pallas_call x1, Pallas kernels: 46 us -> 42 us  [per_device(): pl.pallas_call(lambda *refs: kernel(norm, strips, *refs), name='covarianc...]
where the time goes in v2:
time: 43.8 us
  Pallas kernels  42 us (96%)
  other arithmetic  1.76 us (4%)
    pallas_call x1, Pallas kernels, per_device(): pl.pallas_call(lambda *refs: kernel(norm, strips, *refs), name='covarianc...  42 us
    add x1, other arithmetic, per_device(): return a + b  1.76 us

profile of v2, /device:TPU:7, one launch (start us, length us, event | category | flops | bytes accessed | tf_op | source)
XLA Modules:
  0.0 43.8 jit_solution(10555578431150456196)
XLA Ops:
  0.0 42.0 %covariance.1 = (f32[2,32,1024]{2,1,0:T(8,128)}, f32[2,32,1024]{2,1,0:T(8,128)}) custom-call(f32[2,32,1024]{2,1,0:T(8,128)} %refs_0_.1, bf16[16,8,32,1024]{3,2,1,0:T(8,128)(2,1)} %refs_1_.1, s32[32,1024]{1,0:T(8,128)} %refs_2_.1), custom_call_target="tpu_custom_call" | custom-call | tf_op jit(solution)/shard_map/covariance/pallas_call | solution.py:450
  42.0 1.8 %add.3 = f32[2,32,1024]{2,1,0:T(8,128)} add(f32[2,32,1024]{2,1,0:T(8,128)} %get-tuple-element.7, f32[2,32,1024]{2,1,0:T(8,128)} %get-tuple-element.8) | non-fusion elementwise | flops 65536 | bytes 786432 | tf_op jit(solution)/shard_map/add | solution.py:482

commit v3 on v2

--- a/solution.py
+++ b/solution.py
@@ -116,6 +116,10 @@
 
     def send_halos(sl):
         for side, has, turn, _ in sides:
+            @pl.when(turn)
+            def _():
+                to_relay(sl, side).start()
+
             @pl.when(has)
             def _():
                 halo(sl, side, 0).start()
@@ -123,10 +127,6 @@
             @pl.when(jnp.logical_and(has, jnp.logical_not(turn)))
             def _():
                 halo(sl, side, 1).start()
-
-            @pl.when(turn)
-            def _():
-                to_relay(sl, side).start()
 
     def pass_on(sl):
         for side, _, _, relay in sides:

time: 43.8 us -> 41.4 us (0.945)
  Pallas kernels: 42 us -> 39.5 us
    pallas_call x1, Pallas kernels: 42 us -> 39.5 us  [per_device(): pl.pallas_call(lambda *refs: kernel(norm, strips, *refs), name='covarianc...]
where the time goes in v3:
time: 41.4 us; the launch traced here: 41.3 us
  Pallas kernels  39.5 us (95%)
  other arithmetic  1.76 us (4%)
    pallas_call x1, Pallas kernels, per_device(): pl.pallas_call(lambda *refs: kernel(norm, strips, *refs), name='covarianc...  39.5 us
    add x1, other arithmetic, per_device(): return a + b  1.76 us

profile of v3, /device:TPU:7, one launch (start us, length us, event | category | flops | bytes accessed | tf_op | source)
XLA Modules:
  0.0 41.3 jit_solution(16154784639518585081)
XLA Ops:
  0.0 39.5 %covariance.1 = (f32[2,32,1024]{2,1,0:T(8,128)}, f32[2,32,1024]{2,1,0:T(8,128)}) custom-call(f32[2,32,1024]{2,1,0:T(8,128)} %refs_0_.1, bf16[16,8,32,1024]{3,2,1,0:T(8,128)(2,1)} %refs_1_.1, s32[32,1024]{1,0:T(8,128)} %refs_2_.1), custom_call_target="tpu_custom_call" | custom-call | tf_op jit(solution)/shard_map/covariance/pallas_call | solution.py:450
  39.5 1.8 %add.3 = f32[2,32,1024]{2,1,0:T(8,128)} add(f32[2,32,1024]{2,1,0:T(8,128)} %get-tuple-element.7, f32[2,32,1024]{2,1,0:T(8,128)} %get-tuple-element.8) | non-fusion elementwise | flops 65536 | bytes 786432 | tf_op jit(solution)/shard_map/add | solution.py:482
